TPU v7x, 256 devices: a whole 4x4x8 slice. The times are simulated.
256 devices in a mesh: wide: 32 (over x, z_lo, core), narrow: 8 (over y, z_hi).
Axes of the slice: x: 4, y: 4, z: 8 (z_hi: 2, z_lo: 4; z = z_hi * 4 + z_lo), core: 2. Of those that a mesh axis runs over, the one named last changes fastest.
Arguments:
- hidden_in: bfloat16 [2048, 6144], P('wide', 'narrow'), may hold values from -6 to 6
- w_query: bfloat16 [6144, 6144], P('narrow', 'wide'), may hold values from -1 to 1
- w_key: bfloat16 [6144, 6144], P('narrow', 'wide'), may hold values from -1 to 1
- w_value: bfloat16 [6144, 6144], P('narrow', 'wide'), may hold values from -0.078125 to 0.078125
- qkv_bias: float32 [3, 6144], P(None, 'wide'), may hold values from -3 to 3
- w_up: bfloat16 [6144, 24576], P('narrow', 'wide'), may hold values from -0.078125 to 0.078125
- up_bias: float32 [24576], P('wide'), may hold values from -3 to 3
- w_attn_out: bfloat16 [6144, 6144], P('wide', 'narrow'), may hold values from -0.078125 to 0.078125
- w_down: bfloat16 [24576, 6144], P('wide', 'narrow'), may hold values from -0.0390625 to 0.0390625
- out_bias: float32 [6144], P('narrow'), may hold values from -3 to 3
- norm_gain: float32 [2, 6144], P(None, 'narrow'), may hold values from 0.5 to 1.5
- norm_bias: float32 [2, 6144], P(None, 'narrow'), may hold values from -2 to 2
- seq_lens: int32 [8], replicated, may hold values from 1 to 1024, 2048 in all
- sink_count: int32 [8], replicated, may hold values from 1 to 64, as said below
- page_table: int32 [128], replicated, may hold values from 0 to 127, each once
Outputs:
- hidden_out: bfloat16 [2048, 6144], P('wide', 'narrow')
- paged_cache: bfloat16 [2, 128, 16, 6144], P(None, 'narrow', None, 'wide')
Inputs may be any that keep to these rules, and one draw needn't show every extreme that they name: `seq_lens`: the lengths are positive, add up to 2048, and the longest is exactly 1024. `sink_count`: some sequence has exactly 64 sink tokens. `page_table`: every slot is named by exactly one page.
All inputs are finite; a program needn't handle non-finite values.
Results may differ from a plain program's by a relative error of at most 0.02.
Values may be sent and summed in bfloat16 or wider, within the bound.
A program may use at most 64 MiB of HBM per device.

v0:
```python
import jax
import jax.numpy as jnp
from jax import lax
from jax.sharding import PartitionSpec as P

D = 6144
HEAD_DIM = 96
ROTARY = 24
PAGE = 16


def segment_info(token_index, seq_lens, sink_count):
    seq_ends = jnp.cumsum(seq_lens)
    seq_starts = seq_ends - seq_lens
    inside = (token_index[:, None] >= seq_starts[None, :]) & (
        token_index[:, None] < seq_ends[None, :]
    )
    member = inside.astype(jnp.int32)
    seq_number = jnp.arange(seq_lens.shape[0], dtype=jnp.int32)
    segment = jnp.sum(member * seq_number[None, :], axis=1)
    position = token_index - jnp.sum(member * seq_starts[None, :], axis=1)
    sink_limit = jnp.sum(member * sink_count[None, :], axis=1)
    return (segment, position, sink_limit)


def rotate(values, position):
    half_rot = ROTARY // 2
    freq_index = jnp.arange(half_rot, dtype=jnp.float32)
    inverse = jnp.power(jnp.float32(10000.0), -2.0 * freq_index / ROTARY)
    angles = position.astype(jnp.float32)[:, None] * inverse[None, :]
    cosine = jnp.cos(angles)[:, None, :]
    sine_part = jnp.sin(angles)[:, None, :]
    first_half = values[..., :half_rot]
    second_half = values[..., half_rot:ROTARY]
    return jnp.concatenate(
        [
            first_half * cosine - second_half * sine_part,
            second_half * cosine + first_half * sine_part,
            values[..., ROTARY:],
        ],
        axis=-1,
    )


def local(
    hidden_in,
    w_query,
    w_key,
    w_value,
    qkv_bias,
    w_up,
    up_bias,
    w_attn_out,
    w_down,
    out_bias,
    norm_gain,
    norm_bias,
    seq_lens,
    sink_count,
    page_table,
):
    wide_count = lax.axis_size("wide")
    narrow_count = lax.axis_size("narrow")
    narrow_index = lax.axis_index("narrow")
    tok_local, feat_local = hidden_in.shape
    sub_rows = tok_local // narrow_count
    total_tokens = tok_local * wide_count
    query_rows = wide_count * sub_rows
    head_cols = w_query.shape[1]
    heads_local = head_cols // HEAD_DIM
    as_float = hidden_in.astype(jnp.float32)
    partial_sum = jnp.sum(as_float, axis=1)
    partial_square = jnp.sum(as_float * as_float, axis=1)
    total_sum, total_square = lax.psum((partial_sum, partial_square), "narrow")
    average = total_sum / D
    variance = total_square / D - average * average
    scaled = (as_float - average[:, None]) * lax.rsqrt(variance + 1e-05)[:, None]
    attn_normed = (scaled * norm_gain[0] + norm_bias[0]).astype(jnp.bfloat16)
    mlp_normed = (scaled * norm_gain[1] + norm_bias[1]).astype(jnp.bfloat16)
    stacked = jnp.stack([attn_normed, mlp_normed]).reshape(2, narrow_count, sub_rows, feat_local)
    gathered = lax.all_gather(stacked, "wide", axis=2, tiled=True).reshape(
        2, total_tokens, feat_local
    )
    local_order = jnp.arange(query_rows, dtype=jnp.int32)
    local_tokens = (
        local_order // sub_rows * tok_local + narrow_index * sub_rows + local_order % sub_rows
    )
    local_seg, local_pos, local_sink = segment_info(local_tokens, seq_lens, sink_count)
    all_order = jnp.arange(total_tokens, dtype=jnp.int32)
    all_tokens = (
        all_order % query_rows // sub_rows * tok_local
        + all_order // query_rows * sub_rows
        + all_order % sub_rows
    )
    all_seg, all_pos, all_sink = segment_info(all_tokens, seq_lens, sink_count)
    qkv_weight = jnp.concatenate([w_query, w_key, w_value], axis=1)
    attn_part = gathered[0]
    mlp_part = gathered[1]
    summed = lax.psum_scatter(
        jnp.concatenate(
            [
                jnp.dot(attn_part, qkv_weight, preferred_element_type=jnp.float32),
                jnp.dot(mlp_part, w_up, preferred_element_type=jnp.float32),
            ],
            axis=1,
        ).astype(jnp.bfloat16),
        "narrow",
        scatter_dimension=0,
        tiled=True,
    ).astype(jnp.float32)
    query_sum = summed[:, :head_cols]
    key_sum = summed[:, head_cols : 2 * head_cols]
    value_sum = summed[:, 2 * head_cols : 3 * head_cols]
    unit_sum = summed[:, 3 * head_cols :]
    keys_local = (
        rotate((key_sum + qkv_bias[1]).reshape(query_rows, heads_local, HEAD_DIM), local_pos)
        .astype(jnp.bfloat16)
        .reshape(query_rows, head_cols)
    )
    values_local = (value_sum + qkv_bias[2]).astype(jnp.bfloat16)
    all_keys, all_values = (
        lax.all_gather(keys_local, "narrow", axis=0, tiled=True),
        lax.all_gather(values_local, "narrow", axis=0, tiled=True),
    )
    queries = rotate(
        (query_sum + qkv_bias[0]).reshape(query_rows, heads_local, HEAD_DIM), local_pos
    ).astype(jnp.bfloat16)
    hidden_units = jax.nn.gelu(unit_sum + up_bias, approximate=False).astype(jnp.bfloat16)
    window_span = total_tokens // 16
    allowed = (local_seg[:, None] == all_seg[None, :]) & (all_pos[None, :] <= local_pos[:, None])
    allowed = allowed & (
        (local_pos[:, None] - all_pos[None, :] < window_span)
        | (all_pos[None, :] < local_sink[:, None])
    )
    key_heads = all_keys.reshape(total_tokens, heads_local, HEAD_DIM)
    value_heads = all_values.reshape(total_tokens, heads_local, HEAD_DIM)
    scores = jnp.einsum("qhd,khd->hqk", queries, key_heads, preferred_element_type=jnp.float32) * (
        1.0 / HEAD_DIM**0.5
    )
    masked = jnp.where(allowed[None], scores, jnp.float32(-1e30))
    top_score = jnp.max(masked, axis=2, keepdims=True)
    weights = jnp.exp(masked - top_score)
    probs = (weights / jnp.sum(weights, axis=2, keepdims=True)).astype(jnp.bfloat16)
    attended = (
        jnp.einsum("hqk,khd->qhd", probs, value_heads, preferred_element_type=jnp.float32)
        .astype(jnp.bfloat16)
        .reshape(query_rows, head_cols)
    )
    full_out, full_down = (
        lax.all_gather(w_attn_out, "narrow", axis=1, tiled=True),
        lax.all_gather(w_down, "narrow", axis=1, tiled=True),
    )
    attn_part = attended
    own_rows = lax.psum_scatter(
        (
            jnp.dot(attn_part, full_out, preferred_element_type=jnp.float32)
            + jnp.dot(hidden_units, full_down, preferred_element_type=jnp.float32)
        ).astype(jnp.bfloat16),
        "wide",
        scatter_dimension=0,
        tiled=True,
    ).astype(jnp.float32)
    combined = lax.all_to_all(
        own_rows.astype(jnp.bfloat16), "narrow", split_axis=1, concat_axis=0, tiled=True
    ).astype(own_rows.dtype)
    hidden_out = (as_float + combined + out_bias).astype(jnp.bfloat16)
    pages_local = page_table.shape[0] // narrow_count
    slot_ids = narrow_index * pages_local + jnp.arange(pages_local, dtype=jnp.int32)
    matches = (page_table[None, :] == slot_ids[:, None]).astype(jnp.int32)
    source_page = jnp.sum(
        matches * jnp.arange(page_table.shape[0], dtype=jnp.int32)[None, :], axis=1
    )
    token_ids = (source_page[:, None] * PAGE + jnp.arange(PAGE, dtype=jnp.int32)[None, :]).reshape(
        -1
    )
    gather_rows = (
        token_ids % tok_local // sub_rows * query_rows
        + token_ids // tok_local * sub_rows
        + token_ids % sub_rows
    )
    cache_keys = jnp.take(all_keys, gather_rows, axis=0).reshape(pages_local, PAGE, head_cols)
    cache_values = jnp.take(all_values, gather_rows, axis=0).reshape(pages_local, PAGE, head_cols)
    paged_cache = jnp.stack([cache_keys, cache_values])
    return (hidden_out, paged_cache)


def solution(mesh):
    in_specs = (
        P("wide", "narrow"),
        P("narrow", "wide"),
        P("narrow", "wide"),
        P("narrow", "wide"),
        P(None, "wide"),
        P("narrow", "wide"),
        P("wide"),
        P("wide", "narrow"),
        P("wide", "narrow"),
        P("narrow"),
        P(None, "narrow"),
        P(None, "narrow"),
        P(),
        P(),
        P(),
    )
    out_specs = (P("wide", "narrow"), P(None, "narrow", None, "wide"))
    return jax.shard_map(local, mesh=mesh, in_specs=in_specs, out_specs=out_specs, check_vma=False)
```

profile of v0, /device:TPU:8, one launch (start us, length us, event | category | flops | bytes accessed | tf_op | source)
XLA Modules:
  0.0 761.1 jit_solution(3944237115686412348)
XLA Ops:
  7.2 0.0 copy-start
  7.2 0.0 all-gather.4.cloned.1.call-start
  7.2 1.1 convert_reduce_fusion
  8.3 31.2 %all-reduce = (f32[64]{0:T(128)S(1)}, f32[64]{0:T(128)S(1)}) all-reduce(f32[64]{0:T(128)S(1)} %get-tuple-element.4, f32[64]{0:T(128)S(1)} %get-tuple-element.3), channel_id=1, replica_groups=mesh['wide'=32,'narrow'=8] {'narrow'}, use_global_device_ids=true, to_apply=%region_3.0 | all-reduce | flops 128 | bytes 1024 | tf_op jit(solution)/shard_map/psum | solution.py:74
  39.6 0.8 slice_reduce_fusion.2
  40.4 1.0 fusion.72
  41.4 0.7 pad_maximum_fusion.2
  42.1 0.0 all-gather.4.cloned.1.call-update
  42.1 0.0 reduce-scatter.3.cloned.1.call-start
  42.2 63.7 %all-gather.4.cloned.1.call-done = bf16[2,8,256,768]{3,2,1,0:T(8,128)(2,1)} async-done(((bf16[2,8,8,768]{3,2,1,0:T(8,128)(2,1)}), bf16[2,8,256,768]{3,2,1,0:T(8,128)(2,1)}) %all-gather.4.cloned.1.call-update) | async-done | bytes 6291472 | tf_op jit(solution)/shard_map/all_gather | solution.py:81
  105.9 3.3 fusion.142
  109.2 0.0 copy-done
  109.2 0.0 copy-start.9
  109.2 0.0 copy-start.10
  109.2 0.0 copy-start.11
  109.2 2.9 convolution_convert_fusion
  112.1 0.0 copy-done.9
  112.2 2.0 convolution_convert_fusion.1
  114.2 2.9 pad_maximum_fusion
  117.1 0.0 reduce-scatter.3.cloned.1.call-update
  117.2 0.0 all-gather.8.cloned.1.call-start
  117.2 0.7 all-gather.8.cloned.1.call-update
  117.9 0.0 all-gather.6.cloned.1.call-start
  118.0 0.5 all-gather.6.cloned.1.call-update
  118.5 0.0 reduce-scatter.5.cloned.1.call-start
  118.6 0.2 reduce-window.8
  118.8 0.1 select_reduce_fusion.5
  118.9 0.1 select_reduce_fusion.1
  119.0 0.0 copy-done.7
  119.0 0.1 multiply_cosine_fusion
  119.2 0.9 fusion.6
  120.1 142.9 %reduce-scatter.3.cloned.1.call-done = bf16[256,1344]{0,1:T(8,128)(2,1)} async-done(((bf16[2048,1344]{0,1:T(8,128)(2,1)}), bf16[256,1344]{0,1:T(8,128)(2,1)}) %reduce-scatter.3.cloned.1.call-update) | async-done | bytes 688144 | tf_op jit(solution)/shard_map/reduce_scatter | solution.py:99
  262.9 1.2 convert_element_type.65
  264.1 1.1 copy-done.2
  265.2 0.8 slice_add_fusion.2
  266.0 0.6 slice.120
  266.7 0.6 subtract_convert_fusion.1
  267.3 0.1 copy.20
  267.4 76.0 %all_gather.17 = bf16[2048,192]{1,0:T(8,128)(2,1)S(1)} all-gather(bf16[256,192]{1,0:T(8,128)(2,1)S(1)} %copy.20), channel_id=1, replica_groups=mesh['wide'=32,'narrow'=8] {'narrow'}, dimensions={0}, use_global_device_ids=true | all-gather | bytes 884736 | tf_op jit(solution)/shard_map/all_gather | solution.py:122
  343.5 0.5 copy.21
  344.0 3.3 fusion.144
  347.2 0.0 copy-done.4
  347.2 65.6 %all_gather.16 = bf16[2048,192]{0,1:T(8,128)(2,1)S(1)} all-gather(bf16[256,192]{0,1:T(8,128)(2,1)} %get-tuple-element.24), channel_id=1, replica_groups=mesh['wide'=32,'narrow'=8] {'narrow'}, dimensions={0}, use_global_device_ids=true | all-gather | bytes 884736 | tf_op jit(solution)/shard_map/all_gather | solution.py:123
  412.9 4.1 fusion.9
  416.9 86.6 %all-gather.8.cloned.1.call-done = bf16[768,6144]{1,0:T(8,128)(2,1)} async-done(((bf16[768,768]{1,0:T(8,128)(2,1)}), bf16[768,6144]{1,0:T(8,128)(2,1)}) %all-gather.8.cloned.1.call-update) | async-done | bytes 9437200 | tf_op jit(solution)/shard_map/all_gather | solution.py:151
  503.5 11.0 %fusion.27 = f32[256,6144]{1,0:T(8,128)} fusion(bf16[768,6144]{1,0:T(8,128)(2,1)} %all-gather.8.cloned.1.call-done, f32[256,1344]{0,1:T(8,128)} %copy-done.2, f32[768]{0:T(1024)} %param.23), kind=kOutput, calls=%fused_computation.46 | convolution fusion | flops 2428895232 | bytes 16519168 | tf_op jit(solution)/shard_map/dot_general | solution.py:157
  514.6 70.8 %all-gather.6.cloned.1.call-done = bf16[192,6144]{1,0:T(8,128)(2,1)} async-done(((bf16[192,768]{1,0:T(8,128)(2,1)}), bf16[192,6144]{1,0:T(8,128)(2,1)}) %all-gather.6.cloned.1.call-update) | async-done | bytes 2359312 | tf_op jit(solution)/shard_map/all_gather | solution.py:150
  585.3 6.2 fusion.1
  591.5 0.0 reduce-scatter.5.cloned.1.call-update
  591.6 0.0 copy-start.3
  591.6 0.0 copy-start.6
  591.6 0.6 copy-done.13
  592.2 0.2 select_reduce_fusion.2
  592.4 0.1 iota_add_fusion
  592.4 0.1 add.317
  592.6 1.4 copy.22
  594.0 1.2 gather_fusion
  595.2 1.2 gather_fusion.1
  596.3 141.5 %reduce-scatter.5.cloned.1.call-done = bf16[8,6144]{1,0:T(8,128)(2,1)} async-done(((bf16[256,6144]{1,0:T(8,128)(2,1)}), bf16[8,6144]{1,0:T(8,128)(2,1)}) %reduce-scatter.5.cloned.1.call-update) | async-done | bytes 98320 | tf_op jit(solution)/shard_map/reduce_scatter | solution.py:154
  737.9 7.2 all-to-all-start
  745.1 0.1 broadcast_select_fusion.1
  745.2 0.7 pad_maximum_fusion.1
  745.9 8.0 %all-to-all-done = bf16[8,8,768]{2,0,1:T(8,128)(2,1)S(1)} async-done(((bf16[8,8,768]{2,0,1:T(8,128)(2,1)}), bf16[8,8,768]{2,0,1:T(8,128)(2,1)S(1)}, u32[]{:S(2)}, u32[]{:S(2)}) %all-to-all-start) | async-done | bytes 98336 | tf_op jit(solution)/shard_map/all_to_all | solution.py:163
  753.9 0.7 fusion.69
  (30 shorter events, 0.2 us)
Async XLA Ops:
  7.2 102.0 %copy-start = (bf16[768,768]{1,0:T(8,128)(2,1)S(1)}, bf16[768,768]{1,0:T(8,128)(2,1)}, u32[]{:S(2)}) copy-start(bf16[768,768]{1,0:T(8,128)(2,1)} %param.22) | copy-start | bytes 3538948
  7.2 98.7 %all-gather.4.cloned.1.call-start = ((), (), s32[]{:S(2)}) async-start(), calls=%async_computation.3 | async-start | bytes 6488064 | tf_op jit(solution)/shard_map/all_gather | solution.py:81
  42.1 220.8 %reduce-scatter.3.cloned.1.call-start = ((), (), s32[]{:S(2)}) async-start(), calls=%async_computation.4 | async-start | bytes 6193152 | tf_op jit(solution)/shard_map/reduce_scatter | solution.py:99
  109.2 3.0 copy-start.9
  109.2 3.0 copy-start.10
  109.2 3.0 copy-start.11
  117.1 1.4 copy-start.12
  117.1 1.6 copy-start.8
  117.1 1.9 copy-start.7
  117.2 386.4 %all-gather.8.cloned.1.call-start = ((), (), s32[]{:S(2)}) async-start(), calls=%async_computation.6 | async-start | bytes 10616832 | tf_op jit(solution)/shard_map/all_gather | solution.py:151
  117.9 467.4 %all-gather.6.cloned.1.call-start = ((), (), s32[]{:S(2)}) async-start(), calls=%async_computation.5 | async-start | bytes 2654208 | tf_op jit(solution)/shard_map/all_gather | solution.py:150
  118.5 619.4 %reduce-scatter.5.cloned.1.call-start = ((), (), s32[]{:S(2)}) async-start(), calls=%async_computation.7 | async-start | bytes 3244032 | tf_op jit(solution)/shard_map/reduce_scatter | solution.py:154
  264.1 1.1 copy-start.2
  344.0 3.3 copy-start.4
  412.9 4.1 copy-start.1
  416.9 168.4 %copy-start.5 = (bf16[2,96,256]{2,1,0:T(8,128)(2,1)S(1)}, bf16[2,96,256]{2,1,0:T(8,128)(2,1)}, u32[]{:S(2)}) copy-start(bf16[2,96,256]{2,1,0:T(8,128)(2,1)} %fusion.9) | copy-start | bytes 294916
  591.5 0.7 copy-start.13
  591.6 162.4 %copy-start.3 = (bf16[64,768]{1,0:T(8,128)(2,1)S(1)}, bf16[64,768]{1,0:T(8,128)(2,1)}, u32[]{:S(2)}) copy-start(bf16[64,768]{1,0:T(8,128)(2,1)} %param.17) | copy-start | bytes 294916
  591.6 162.4 %copy-start.6 = (f32[768]{0:T(1024)S(1)}, f32[768]{0:T(1024)}, u32[]{:S(2)}) copy-start(f32[768]{0:T(1024)} %param.26) | copy-start | bytes 9220
  737.9 16.1 %all-to-all-start = ((bf16[8,8,768]{2,0,1:T(8,128)(2,1)}), bf16[8,8,768]{2,0,1:T(8,128)(2,1)S(1)}, u32[]{:S(2)}, u32[]{:S(2)}) async-start(bf16[8,8,768]{2,0,1:T(8,128)(2,1)} %bitcast.49), calls=%async_computation.2 | async-start | bytes 196608 | tf_op jit(solution)/shard_map/all_to_all | solution.py:163
Sparse Core Ops, SparseCore 0:
  42.2 63.6 all-gather.3
  117.3 145.6 reduce-scatter.2
  265.9 237.5 all-gather.7
  506.4 78.9 all-gather.5
  591.7 146.1 reduce-scatter.4
where the time goes:
time: 762 us; the launch traced here: 761 us
  waiting for transfers between devices  515 us (68%)
  blocking collectives  173 us (23%)
  matrix products  29.5 us (4%)
  between operations  14.1 us (2%)
  other arithmetic  11.6 us (2%)
  local copies, waits for them, and re-layouts  10.9 us (1%)
    reduce_scatter x1, waiting for transfers between devices, local(): lax.psum_scatter(jnp.concatenate([jnp.dot(attn_part, qkv_weight, preferre...  143 us
    reduce_scatter x1, waiting for transfers between devices, local(): lax.psum_scatter((jnp.dot(attn_part, full_out, preferred_element_type=jnp...  142 us
    all_gather x1, waiting for transfers between devices, local(): lax.all_gather(w_down, 'narrow', axis=1, tiled=True)  86.6 us
    all_gather x1, blocking collectives, local(): lax.all_gather(keys_local, 'narrow', axis=0, tiled=True)  76 us
    all_gather x1, waiting for transfers between devices, local(): lax.all_gather(w_attn_out, 'narrow', axis=1, tiled=True)  70.8 us
    all_gather x1, blocking collectives, local(): lax.all_gather(values_local, 'narrow', axis=0, tiled=True)  65.6 us
    all_gather x1, waiting for transfers between devices, local(): lax.all_gather(stacked, 'wide', axis=2, tiled=True)  63.7 us
    psum x1, blocking collectives, local(): total_sum, total_square = lax.psum((partial_sum, partial_square), 'narrow')  31.2 us
  transfers between devices with their start and end apart: 6, of which 6 were waited for; matrix products, arithmetic and copies ran while one was open for 4% of the time, Pallas kernels for 0%

commit v1 on v0

v1 whole, which is shorter than its diff:
```python
import functools

import jax
import jax.numpy as jnp
from jax import lax
from jax.experimental import pallas as pl
from jax.experimental.pallas import tpu as pltpu
from jax.sharding import PartitionSpec as P

D = 6144
HEAD_DIM = 96
ROTARY = 24
PAGE = 16
WINDOW = 128
MOST_SINKS = 64
MESH = pl.DeviceIdType.MESH
F32 = jnp.float32
BF16 = jnp.bfloat16
VM = pltpu.VMEM
DMA = pltpu.SemaphoreType.DMA
QKV_PAD = 640
HALF_FF = 384


class Place:
    def __init__(self):
        wide = lax.axis_index("wide")
        narrow = lax.axis_index("narrow")
        self.x, self.zl, self.c = wide // 8, (wide // 2) % 4, wide % 2
        self.y, self.zh = narrow // 2, narrow % 2
        self.wide, self.narrow = wide, narrow

    def in_wide(self, dx, dz, dc):
        return lax.rem(self.x + dx, 4) * 8 + lax.rem(self.zl + dz, 4) * 2 + lax.rem(self.c + dc, 2)

    def in_narrow(self, dy, dh):
        return lax.rem(self.y + dy, 4) * 2 + lax.rem(self.zh + dh, 2)

    def wide_peer(self, dx, dz, dc):
        return {"wide": self.in_wide(dx, dz, dc), "narrow": self.narrow}

    def narrow_peer(self, dy, dh):
        return {"wide": self.wide, "narrow": self.in_narrow(dy, dh)}


def greet(peers):
    barrier = pltpu.get_barrier_semaphore()
    for peer in peers:
        pl.semaphore_signal(barrier, inc=1, device_id=peer, device_id_type=MESH)
    pl.semaphore_wait(barrier, len(peers))


def send(src, dst, send_sem, recv_sem, peer):
    copy = pltpu.make_async_remote_copy(
        src_ref=src,
        dst_ref=dst,
        send_sem=send_sem,
        recv_sem=recv_sem,
        device_id=peer,
        device_id_type=MESH,
    )
    copy.start()
    return copy


def arrived(dst, sem, peer):
    pltpu.make_async_remote_copy(
        src_ref=dst, dst_ref=dst, send_sem=sem, recv_sem=sem, device_id=peer, device_id_type=MESH
    ).wait_recv()


WIDE_HOPS = [(1, 0, 0), (2, 0, 0), (3, 0, 0), (0, 1, 0), (0, 2, 0), (0, 3, 0), (0, 0, 1)]


def slot(a, k, c):
    return (a % 4) * 8 + (k % 4) * 2 + c % 2


def project_kernel(
    hidden_ref,
    gain_ref,
    shift_ref,
    w_qkv_ref,
    w_up_ref,
    qkv_bias_ref,
    up_bias_ref,
    cos_ref,
    sin_lo_ref,
    sin_hi_ref,
    out_q,
    out_u1,
    out_u2,
    gathered,
    stats,
    stats_part,
    normed,
    part_q,
    part_u1,
    part_u2,
    *rest,
):
    n_ch = 3
    outs = [out_q, out_u1, out_u2]
    parts = [part_q, part_u1, part_u2]
    mids = [rest[4 * i : 4 * i + 4] for i in range(n_ch)]
    rest = rest[4 * n_ch :]
    wide_send, wide_recv, stat_send, stat_recv, sn_send, sn_recv, ch_send, ch_recv = rest
    me = Place()
    rows = 64
    greet(
        [me.wide_peer(*hop) for hop in WIDE_HOPS]
        + [me.narrow_peer(dy, dh) for dy in range(4) for dh in range(2) if dy or dh]
    )
    open_copies = []
    counts = {"wide": 0, "stat": 0}

    def push(kind, block, rel, hop, own):
        buf, ss, rs = (
            (gathered, wide_send, wide_recv) if kind == "wide" else (stats, stat_send, stat_recv)
        )
        i = counts[kind]
        counts[kind] = i + 1
        index = me.in_wide(*rel)
        src = hidden_ref if own and kind == "wide" else buf.at[index]
        there = slot(rel[0] - hop[0], rel[1] - hop[1], rel[2] - hop[2])
        open_copies.append(
            send(src, buf.at[index], ss.at[i], rs.at[there], me.wide_peer(*hop))
        )

    def wait_block(kind, rel):
        buf, rs = (gathered, wide_recv) if kind == "wide" else (stats, stat_recv)
        arrived(buf.at[me.in_wide(*rel)], rs.at[slot(*rel)], me.wide_peer(0, 0, 1))

    def normalise(block, index):
        as_float = block.astype(F32)
        line = stats[index][0:1, :]
        lane = lax.broadcasted_iota(jnp.int32, (rows, 128), 1)
        row = lax.broadcasted_iota(jnp.int32, (rows, 128), 0)
        average = jnp.sum(jnp.where(lane == row, line, 0.0), axis=1, keepdims=True)
        inverse = jnp.sum(jnp.where(lane == row + rows, line, 0.0), axis=1, keepdims=True)
        scaled = (as_float - average) * inverse
        for i in range(2):
            normed[i, index] = (scaled * gain_ref[i : i + 1, :] + shift_ref[i : i + 1, :]).astype(BF16)

    for hop in WIDE_HOPS:
        push("wide", None, (0, 0, 0), hop, True)

    as_float = hidden_ref[...].astype(F32)
    ones = jnp.ones((8, as_float.shape[1]), F32)

    def row_sums(v):
        return lax.dot_general(
            ones, v, (((1,), (1,)), ((), ())), precision=lax.Precision.HIGHEST,
            preferred_element_type=F32,
        )

    stats_part[me.narrow] = jnp.concatenate([row_sums(as_float), row_sums(as_float * as_float)], axis=1)
    i = 0
    for dy in range(4):
        for dh in range(2):
            if dy or dh:
                there = ((-dy) % 4) * 2 + (-dh) % 2
                open_copies.append(
                    send(
                        stats_part.at[me.narrow], stats_part.at[me.narrow],
                        sn_send.at[i], sn_recv.at[there], me.narrow_peer(dy, dh),
                    )
                )
                i += 1
    for dy in range(4):
        for dh in range(2):
            if dy or dh:
                arrived(
                    stats_part.at[me.in_narrow(dy, dh)], sn_recv.at[dy * 2 + dh], me.narrow_peer(dy, dh)
                )
    total = stats_part[0]
    for i in range(1, 8):
        total = total + stats_part[i]
    average = total[:, :rows] / D
    variance = total[:, rows:] / D - average * average
    stats[me.wide] = jnp.concatenate([average, lax.rsqrt(variance + 1e-05)], axis=1)
    for hop in WIDE_HOPS:
        push("stat", None, (0, 0, 0), hop, True)
    normalise(hidden_ref[...], me.wide)

    x_hops = [(1, 0, 0), (3, 0, 0), (2, 0, 0)]
    core = (0, 0, 1)
    ready = []
    for k in (1, 3, 2):
        rel = (0, k, 0)
        for kind in ("stat", "wide"):
            wait_block(kind, rel)
            for hop in x_hops:
                push(kind, None, rel, hop, False)
            push(kind, None, rel, core, False)
        normalise(gathered[me.in_wide(*rel)], me.in_wide(*rel))
    for k in (0, 1, 3, 2):
        for a in (1, 3, 2):
            rel = (a, k, 0)
            for kind in ("stat", "wide"):
                wait_block(kind, rel)
                push(kind, None, rel, core, False)
            normalise(gathered[me.in_wide(*rel)], me.in_wide(*rel))
    for k in (0, 1, 3, 2):
        for a in (0, 1, 3, 2):
            rel = (a, k, 1)
            for kind in ("stat", "wide"):
                wait_block(kind, rel)
            normalise(gathered[me.in_wide(*rel)], me.in_wide(*rel))

    def rows_of(which, owner):
        return normed[which, pl.ds(owner * 4, 4)].reshape(256, normed.shape[-1])

    @pl.loop(0, 8)
    def _(owner):
        part_q[owner] = jnp.dot(rows_of(0, owner), w_qkv_ref[...], preferred_element_type=F32).astype(BF16)

    n_sent = [0] * n_ch
    up, down = me.narrow_peer(1, 0), me.narrow_peer(3, 0)
    across = me.narrow_peer(0, 1)
    ra, rb = pl.ds(0, 128), pl.ds(128, 128)

    def put(ch, src, dst, sem, peer):
        i = n_sent[ch]
        n_sent[ch] = i + 1
        open_copies.append(send(src, dst, ch_send.at[ch, i], ch_recv.at[ch, sem], peer))

    def got(ch, dst, sem):
        arrived(dst, ch_recv.at[ch, sem], up)

    def scatter_first(ch, h):
        part, (first, side, _, _) = parts[ch], mids[ch]
        far, nxt, prv = me.in_narrow(2, h), me.in_narrow(1, h), me.in_narrow(3, h)
        put(ch, part.at[far, ra], first.at[h, 0], 6 * h + 0, up)
        put(ch, part.at[far, rb], first.at[h, 1], 6 * h + 1, down)
        put(ch, part.at[nxt, rb], side.at[h, 0, rb], 6 * h + 2, up)
        put(ch, part.at[prv, ra], side.at[h, 1, ra], 6 * h + 3, down)

    def scatter_second(ch, h):
        part, (first, side, _, _) = parts[ch], mids[ch]
        nxt, prv = me.in_narrow(1, h), me.in_narrow(3, h)
        got(ch, first.at[h, 0], 6 * h + 0)
        part[nxt, ra] = (part[nxt, ra].astype(F32) + first[h, 0].astype(F32)).astype(BF16)
        put(ch, part.at[nxt, ra], side.at[h, 0, ra], 6 * h + 4, up)
        got(ch, first.at[h, 1], 6 * h + 1)
        part[prv, rb] = (part[prv, rb].astype(F32) + first[h, 1].astype(F32)).astype(BF16)
        put(ch, part.at[prv, rb], side.at[h, 1, rb], 6 * h + 5, down)

    def sum_of(ch, h):
        part, (first, side, _, _) = parts[ch], mids[ch]
        got(ch, side.at[h, 0, rb], 6 * h + 2)
        got(ch, side.at[h, 1, ra], 6 * h + 3)
        got(ch, side.at[h, 0, ra], 6 * h + 4)
        got(ch, side.at[h, 1, rb], 6 * h + 5)
        own = me.in_narrow(0, h)
        return part[own].astype(F32) + side[h, 0].astype(F32) + side[h, 1].astype(F32)

    def scatter_across(ch):
        zbuf = mids[ch][2]
        zbuf[0] = sum_of(ch, 1).astype(BF16)
        put(ch, zbuf.at[0], zbuf.at[1], 12, across)

    def finish(ch):
        zbuf = mids[ch][2]
        summed = sum_of(ch, 0)
        got(ch, zbuf.at[1], 12)
        summed = summed + zbuf[1].astype(F32)
        if ch == 0:
            u = summed + qkv_bias_ref[...]
            u = (
                u * cos_ref[...]
                + pltpu.roll(u, QKV_PAD - ROTARY // 2, 1) * sin_lo_ref[...]
                + pltpu.roll(u, ROTARY // 2, 1) * sin_hi_ref[...]
            )
        else:
            u = summed + up_bias_ref[ch - 1 : ch, :]
            u = 0.5 * u * (1.0 + lax.erf(u * (0.5**0.5)))
        out = outs[ch]
        out[me.narrow] = u.astype(BF16)
        mine = out.at[me.narrow]
        put(ch, mine, mine, 13, across)
        put(ch, mine, mine, 14, up)
        put(ch, mine, mine, 15, down)

    def relay_half(ch, h):
        out = outs[ch]
        below, above = me.in_narrow(3, h), me.in_narrow(1, h)
        got(ch, out.at[below], 14 + 4 * h)
        put(ch, out.at[below, ra], out.at[below, ra], 16 + 4 * h, up)
        got(ch, out.at[above], 15 + 4 * h)
        put(ch, out.at[above, rb], out.at[above, rb], 17 + 4 * h, down)

    def relay_across(ch):
        block = outs[ch].at[me.in_narrow(0, 1)]
        got(ch, block, 13)
        put(ch, block, block, 18, up)
        put(ch, block, block, 19, down)

    def gather_last(ch):
        for h in range(2):
            far = outs[ch].at[me.in_narrow(2, h)]
            got(ch, far.at[ra], 16 + 4 * h)
            got(ch, far.at[rb], 17 + 4 * h)

    scatter_first(0, 1)
    scatter_first(0, 0)

    @pl.loop(0, 8)
    def _(owner):
        up_part = jnp.dot(rows_of(1, owner), w_up_ref[...], preferred_element_type=F32).astype(BF16)
        part_u1[owner] = up_part[:, :HALF_FF]
        part_u2[owner] = up_part[:, HALF_FF:]

    scatter_second(0, 1)
    scatter_second(0, 0)
    scatter_first(1, 1)
    scatter_first(1, 0)
    scatter_across(0)
    scatter_second(1, 1)
    scatter_second(1, 0)
    scatter_first(2, 1)
    scatter_first(2, 0)
    finish(0)
    scatter_across(1)
    scatter_second(2, 1)
    scatter_second(2, 0)
    relay_half(0, 0)
    relay_across(0)
    finish(1)
    scatter_across(2)
    relay_half(0, 1)
    relay_half(1, 0)
    relay_across(1)
    finish(2)
    relay_half(1, 1)
    relay_half(2, 0)
    relay_across(2)
    relay_half(2, 1)
    for ch in range(n_ch):
        gather_last(ch)
    for copy in open_copies:
        copy.wait_send()


def project(hidden, gain, shift, w_qkv, w_up, qkv_bias, up_bias, cos, sin_lo, sin_hi):
    width = hidden.shape[1]
    cols = [QKV_PAD, HALF_FF, HALF_FF]
    mids = []
    for c in cols:
        mids += [VM((2, 2, 128, c), BF16), VM((2, 2, 256, c), BF16), VM((2, 256, c), BF16), VM((8, 128), F32)]
    return pl.pallas_call(
        project_kernel,
        out_shape=[jax.ShapeDtypeStruct((8, 256, c), BF16) for c in cols],
        in_specs=[pl.BlockSpec(memory_space=VM)] * 10,
        out_specs=[pl.BlockSpec(memory_space=VM)] * 3,
        scratch_shapes=[
            VM((32, 64, width), BF16),
            VM((32, 8, 128), F32),
            VM((8, 8, 128), F32),
            VM((2, 32, 64, width), BF16),
        ]
        + [VM((8, 256, c), BF16) for c in cols]
        + mids
        + [DMA((31,)), DMA((32,)), DMA((31,)), DMA((32,)), DMA((7,)), DMA((8,)), DMA((3, 22)), DMA((3, 22))],
        compiler_params=pltpu.CompilerParams(
            collective_id=0, has_side_effects=True, vmem_limit_bytes=56 << 20
        ),
        name="project",
    )(hidden, gain, shift, w_qkv, w_up, qkv_bias, up_bias, cos, sin_lo, sin_hi)


def attend_kernel(lens, sinks, pages, qkv_ref, out_ref, cache_ref):
    block = pl.program_id(0)
    queries, span, tail = 256, 384, 128
    total = qkv_ref.shape[0]
    first = block * queries
    width = out_ref.shape[1]

    def of_sequence(token):
        end = 0
        start = jnp.zeros_like(token)
        sink = jnp.zeros_like(token) + sinks[0]
        for s in range(8):
            end = end + lens[s]
            after = token >= end
            start = jnp.where(after, end, start)
            if s < 7:
                sink = jnp.where(after, sinks[s + 1], sink)
        return start, start + sink

    query = first + lax.broadcasted_iota(jnp.int32, (queries, 1), 0)
    start, sink_end = of_sequence(query)
    near = pl.multiple_of(jnp.maximum(first - WINDOW, 0), WINDOW)
    head_start, _ = of_sequence(first)
    far = pl.multiple_of(jnp.minimum(head_start // 16 * 16, total - tail), 16)
    near_key = near + lax.broadcasted_iota(jnp.int32, (1, span), 1)
    far_key = far + lax.broadcasted_iota(jnp.int32, (1, tail), 1)

    def allowed(key):
        return (key >= start) & (key <= query) & ((query - key < WINDOW) | (key < sink_end))

    near_ok = allowed(near_key)
    far_ok = allowed(far_key) & (far_key < near)
    mask = jnp.concatenate([near_ok, far_ok], axis=1)
    q = qkv_ref[pl.ds(first, queries), :][:, :width]
    near_rows = qkv_ref[pl.ds(near, span), :]
    far_rows = qkv_ref[pl.ds(far, tail), :]
    keys = jnp.concatenate([near_rows[:, width : 2 * width], far_rows[:, width : 2 * width]], axis=0)
    values = jnp.concatenate(
        [near_rows[:, 2 * width : 3 * width], far_rows[:, 2 * width : 3 * width]], axis=0
    )
    lane = lax.broadcasted_iota(jnp.int32, (queries, width), 1)
    result = None
    for head in range(width // HEAD_DIM):
        in_head = (lane >= head * HEAD_DIM) & (lane < (head + 1) * HEAD_DIM)
        masked_q = jnp.where(in_head, q, jnp.zeros_like(q))
        scores = lax.dot_general(
            masked_q, keys, (((1,), (1,)), ((), ())), preferred_element_type=F32
        ) * (1.0 / HEAD_DIM**0.5)
        scores = jnp.where(mask, scores, F32(-1e30))
        weights = jnp.exp(scores - jnp.max(scores, axis=1, keepdims=True))
        probs = (weights / jnp.sum(weights, axis=1, keepdims=True)).astype(BF16)
        got = jnp.dot(probs, values, preferred_element_type=F32)
        result = got if result is None else jnp.where(in_head, got, result)
    out_ref[...] = result.astype(BF16)
    for j in range(2):
        row = pl.multiple_of(pages[block * 2 + j] * PAGE, PAGE)
        page = qkv_ref[pl.ds(row, PAGE), :]
        cache_ref[0, j] = page[:, width : 2 * width]
        cache_ref[1, j] = page[:, 2 * width : 3 * width]


def attend(lens, sinks, pages, qkv, width):
    return pl.pallas_call(
        attend_kernel,
        out_shape=[
            jax.ShapeDtypeStruct((qkv.shape[0], width), BF16),
            jax.ShapeDtypeStruct((2, 16, PAGE, width), BF16),
        ],
        grid_spec=pltpu.PrefetchScalarGridSpec(
            num_scalar_prefetch=3,
            grid=(8,),
            in_specs=[pl.BlockSpec(qkv.shape, lambda b, *_: (0, 0))],
            out_specs=[
                pl.BlockSpec((256, width), lambda b, *_: (b, 0)),
                pl.BlockSpec((2, 2, PAGE, width), lambda b, *_: (0, b, 0, 0)),
            ],
        ),
        name="attend",
    )(lens, sinks, pages, qkv)


def output_kernel(
    att_ref,
    u1_ref,
    u2_ref,
    w_out_ref,
    w_down_ref,
    hidden_ref,
    bias_ref,
    out_ref,
    products,
    core_in,
    halves,
    x_in,
    z_out,
    z_in,
    core_send,
    core_recv,
    x_send,
    x_recv,
    z_send,
    z_recv,
):
    me = Place()
    greet([me.wide_peer(*hop) for hop in WIDE_HOPS])
    open_copies = []
    sibling = me.wide_peer(0, 0, 1)
    width = out_ref.shape[1]
    order = (2, 1, 3, 0)
    for half in range(2):
        for dx in order:
            n = lax.rem(me.x + dx, 4) * 2 + half
            o = jnp.dot(u1_ref[n], w_down_ref[:HALF_FF, :], preferred_element_type=F32)
            o = o + jnp.dot(u2_ref[n], w_down_ref[HALF_FF:, :], preferred_element_type=F32)
            o = o + jnp.dot(att_ref[n], w_out_ref[...], preferred_element_type=F32)
            products[n] = o.astype(BF16).reshape(2, 2, 64, width)
            for j in range(2):
                i = half * 8 + dx * 2 + j
                open_copies.append(
                    send(
                        products.at[n, j, 1 - me.c], core_in.at[n, j], core_send.at[i], core_recv.at[i], sibling
                    )
                )
    for half in range(2):
        for dx in order:
            n = lax.rem(me.x + dx, 4) * 2 + half
            for j in range(2):
                arrived(core_in.at[n, j], core_recv.at[half * 8 + dx * 2 + j], sibling)
            halves[half, dx] = (products[n, :, me.c].astype(F32) + core_in[n].astype(F32)).astype(BF16)
            if dx:
                i = half * 3 + dx - 1
                there = half * 3 + (4 - dx) - 1
                open_copies.append(
                    send(
                        halves.at[half, dx], x_in.at[half, 3 - dx],
                        x_send.at[i], x_recv.at[there], me.wide_peer(dx, 0, 0),
                    )
                )
    for half in range(2):
        total = halves[half, 0].astype(F32)
        for dx in (1, 3, 2):
            arrived(x_in.at[half, dx - 1], x_recv.at[half * 3 + dx - 1], sibling)
            total = total + x_in[half, dx - 1].astype(F32)
        z_out[half] = total.astype(BF16)
        for j in range(2):
            to = half * 2 + j
            peer = {"wide": me.x * 8 + to * 2 + me.c, "narrow": me.narrow}

            @pl.when(me.zl != to)
            def _():
                send(z_out.at[half, j], z_in.at[me.zl], z_send.at[to], z_recv.at[me.zl], peer)

    total = z_out[me.zl // 2, me.zl % 2].astype(F32) + hidden_ref[...].astype(F32) + bias_ref[...]
    for k in range(1, 4):
        source = lax.rem(me.zl + k, 4)
        arrived(z_in.at[source], z_recv.at[source], sibling)
        total = total + z_in[source].astype(F32)
    out_ref[...] = total.astype(BF16)
    for copy in open_copies:
        copy.wait_send()
    for k in range(1, 4):
        to = lax.rem(me.zl + k, 4)
        pltpu.make_async_remote_copy(
            src_ref=z_out.at[to // 2, to % 2], dst_ref=z_in.at[me.zl], send_sem=z_send.at[to],
            recv_sem=z_recv.at[me.zl], device_id=me.wide_peer(0, k, 0), device_id_type=MESH,
        ).wait_send()


def output(att, u1, u2, w_out, w_down, hidden, bias):
    width = hidden.shape[1]
    return pl.pallas_call(
        output_kernel,
        out_shape=jax.ShapeDtypeStruct(hidden.shape, BF16),
        in_specs=[pl.BlockSpec(memory_space=VM)] * 7,
        out_specs=pl.BlockSpec(memory_space=VM),
        scratch_shapes=[
            VM((8, 2, 2, 64, width), BF16),
            VM((8, 2, 64, width), BF16),
            VM((2, 4, 2, 64, width), BF16),
            VM((2, 3, 2, 64, width), BF16),
            VM((2, 2, 64, width), BF16),
            VM((4, 64, width), BF16),
            DMA((16,)),
            DMA((16,)),
            DMA((6,)),
            DMA((6,)),
            DMA((4,)),
            DMA((4,)),
        ],
        compiler_params=pltpu.CompilerParams(
            collective_id=1, has_side_effects=True, vmem_limit_bytes=56 << 20
        ),
        name="output",
    )(att, u1, u2, w_out, w_down, hidden, bias)


def rotation_tables(narrow_index, seq_lens):
    token = narrow_index * 256 + jnp.arange(256, dtype=jnp.int32)
    ends = jnp.cumsum(seq_lens)
    after = token[:, None] >= ends[None, :]
    position = token - jnp.sum(jnp.where(after, seq_lens[None, :], 0), axis=1)
    half = ROTARY // 2
    freq_index = jnp.arange(half, dtype=F32)
    inverse = jnp.power(F32(10000.0), -2.0 * freq_index / ROTARY)
    angles = position.astype(F32)[:, None] * inverse[None, :]
    cosine, sine = jnp.cos(angles), jnp.sin(angles)

    def spread(parts, rest):
        head = jnp.concatenate(parts + [jnp.full((256, HEAD_DIM - ROTARY), rest, F32)], axis=1)
        return jnp.concatenate(
            [jnp.tile(head, (1, 4)), jnp.full((256, QKV_PAD - 4 * HEAD_DIM), rest, F32)], axis=1
        )

    none = jnp.zeros_like(sine)
    return spread([cosine, cosine], 1.0), spread([-sine, none], 0.0), spread([none, sine], 0.0)


def local(
    hidden_in,
    w_query,
    w_key,
    w_value,
    qkv_bias,
    w_up,
    up_bias,
    w_attn_out,
    w_down,
    out_bias,
    norm_gain,
    norm_bias,
    seq_lens,
    sink_count,
    page_table,
):
    narrow_index = lax.axis_index("narrow")
    feat, head_cols = w_query.shape
    pad = QKV_PAD - 3 * head_cols
    w_qkv = jnp.concatenate([w_query, w_key, w_value, jnp.zeros((feat, pad), BF16)], axis=1)
    bias = jnp.concatenate([qkv_bias.reshape(1, -1), jnp.zeros((1, pad), F32)], axis=1)
    cos, sin_lo, sin_hi = rotation_tables(narrow_index, seq_lens)
    qkv, u1, u2 = project(
        hidden_in, norm_gain, norm_bias, w_qkv, w_up, bias, up_bias.reshape(2, HALF_FF), cos, sin_lo, sin_hi
    )
    pages_local = page_table.shape[0] // 8
    slot_ids = narrow_index * pages_local + jnp.arange(pages_local, dtype=jnp.int32)
    matches = (page_table[None, :] == slot_ids[:, None]).astype(jnp.int32)
    source_page = jnp.sum(
        matches * jnp.arange(page_table.shape[0], dtype=jnp.int32)[None, :], axis=1
    )
    attended, cache = attend(seq_lens, sink_count, source_page, qkv.reshape(2048, QKV_PAD), head_cols)
    hidden_out = output(
        attended.reshape(8, 256, head_cols), u1, u2, w_attn_out, w_down, hidden_in, out_bias.reshape(1, -1)
    )
    return (hidden_out, cache)


def solution(mesh):
    in_specs = (
        P("wide", "narrow"),
        P("narrow", "wide"),
        P("narrow", "wide"),
        P("narrow", "wide"),
        P(None, "wide"),
        P("narrow", "wide"),
        P("wide"),
        P("wide", "narrow"),
        P("wide", "narrow"),
        P("narrow"),
        P(None, "narrow"),
        P(None, "narrow"),
        P(),
        P(),
        P(),
    )
    out_specs = (P("wide", "narrow"), P(None, "narrow", None, "wide"))
    return jax.shard_map(local, mesh=mesh, in_specs=in_specs, out_specs=out_specs, check_vma=False)
```

time: 762 us -> 216 us (0.28)
  waiting for transfers between devices: 515 us -> 0 us
  Pallas kernels: 0 us -> 201 us
  blocking collectives: 173 us -> 0 us
  matrix products: 29.5 us -> 0 us
  between operations: 14.1 us -> 0.81 us
  other arithmetic: 11.6 us -> 3.87 us
    reduce_scatter x2 -> x0, waiting for transfers between devices: 284 us -> none  [the longest x1 143 us: local(): lax.psum_scatter(jnp.concatenate([jnp.dot(attn_part, qkv_weight, preferre...]
    all_gather x3 -> x0, waiting for transfers between devices: 221 us -> none  [the longest x1 86.6 us: local(): lax.all_gather(w_down, 'narrow', axis=1, tiled=True)]
    pallas_call x0 -> x3, Pallas kernels: none -> 201 us  [the longest x1 146 us: project(): pl.pallas_call(project_kernel, out_shape=[jax.ShapeDtypeStruct((8, 256, c...]
    all_gather x2 -> x0, blocking collectives: 142 us -> none  [the longest x1 76 us: local(): lax.all_gather(keys_local, 'narrow', axis=0, tiled=True)]
    psum x1 -> x0, blocking collectives: 31.2 us -> none  [local(): total_sum, total_square = lax.psum((partial_sum, partial_square), 'narrow')]
    dot_general x5 -> x0, matrix products: 26.2 us -> none  [the longest x1 11 us: local(): jnp.dot(hidden_units, full_down, preferred_element_type=jnp.float32)]
    all_to_all x1 -> x0, waiting for transfers between devices: 8.03 us -> none  [local(): lax.all_to_all(own_rows.astype(jnp.bfloat16), 'narrow', split_axis=1, con...]
  transfers between devices with their start and end apart: 6 -> 0, of which waited for: 6 -> 0; matrix products, arithmetic and copies ran while one was open for 4% -> 0% of each run, Pallas kernels for 0% -> 0%
where the time goes in v1:
time: 216 us; the launch traced here: 213 us
  Pallas kernels  201 us (93%)
  local copies, waits for them, and re-layouts  7.44 us (3%)
  other arithmetic  3.87 us (2%)
    pallas_call x1, Pallas kernels, project(): pl.pallas_call(project_kernel, out_shape=[jax.ShapeDtypeStruct((8, 256, c...  146 us
    pallas_call x1, Pallas kernels, output(): pl.pallas_call(output_kernel, out_shape=jax.ShapeDtypeStruct(hidden.shape...  42.1 us
    pallas_call x1, Pallas kernels, attend(): pl.pallas_call(attend_kernel, out_shape=[jax.ShapeDtypeStruct((qkv.shape[...  13 us

profile of v1, /device:TPU:8, one launch (start us, length us, event | category | flops | bytes accessed | tf_op | source)
XLA Modules:
  0.0 213.0 jit_solution(14913412479498158022)
XLA Ops:
  0.6 0.8 reduce-window.8
  1.5 0.7 select_reduce_fusion
  2.2 0.1 multiply_sine_fusion
  2.4 0.1 pad.12.clone
  2.5 0.1 pad.9.clone
  2.6 0.1 maximum_maximum_fusion.3
  2.7 0.2 copy.29
  2.9 0.9 concatenate.27.cos_ref
  3.8 0.0 copy-start
  3.8 0.2 copy.30
  4.0 0.0 copy-start.1
  4.0 0.9 concatenate.29.sin_lo_ref
  4.9 0.0 copy-start.2
  4.9 0.2 copy.31
  5.1 0.9 concatenate.31.sin_hi_ref
  6.0 0.0 copy-done
  6.0 0.0 copy-start.5
  6.0 0.0 copy-start.3
  6.0 0.2 copy.26
  6.2 0.0 copy-done.1
  6.2 0.2 copy.27
  6.4 0.0 copy-done.2
  6.4 0.2 copy.28
  6.6 0.1 pad.16.clone
  6.6 1.3 maximum_maximum_fusion.w_qkv_ref
  8.0 0.0 copy-done.5
  8.0 0.1 reshape.76
  8.1 0.6 concatenate.25.qkv_bias_ref
  8.7 0.0 copy-done.3
  8.7 0.6 reshape.77.up_bias_ref
  9.2 0.0 copy-start.6
  9.2 145.8 %project.1 = (bf16[8,256,640]{2,1,0:T(8,128)(2,1)}, bf16[8,256,384]{2,1,0:T(8,128)(2,1)}, bf16[8,256,384]{2,1,0:T(8,128)(2,1)}) custom-call(bf16[64,768]{1,0:T(8,128)(2,1)} %hidden_ref.3, f32[2,768]{1,0:T(2,128)} %gain_ref.1, f32[2,768]{1,0:T(2,128)} %shift_ref.1, bf16[768,640]{1,0:T(8,128)(2,1)} %maximum_maximum_fusion.w_qkv_ref, ...), custom_call_target="tpu_custom_call" | custom-call | tf_op jit(solution)/shard_map/project/pallas_call | solution.py:351
  155.1 0.0 copy-start.4
  155.1 0.0 copy-done.6
  155.1 0.7 select_reduce_fusion.1.pages
  155.8 13.0 %attend.1 = (bf16[2048,192]{1,0:T(8,128)(2,1)}, bf16[2,16,16,192]{3,2,1,0:T(8,128)(2,1)}) custom-call(s32[8]{0:T(128)} %lens.1, s32[8]{0:T(128)} %sinks.1, s32[16]{0:T(128)} %select_reduce_fusion.1.pages, bf16[2048,640]{1,0:T(8,128)(2,1)} %bitcast.7), custom_call_target="tpu_custom_call" | custom-call | tf_op jit(solution)/shard_map/attend/pallas_call | solution.py:434
  168.8 0.0 copy-done.4
  168.8 0.6 reshape.82.bias_ref
  169.4 42.1 %output.1 = bf16[64,768]{1,0:T(8,128)(2,1)} custom-call(bf16[8,256,192]{2,1,0:T(8,128)(2,1)} %bitcast.11, bf16[8,256,384]{2,1,0:T(8,128)(2,1)} %get-tuple-element.9.u1_ref, bf16[8,256,384]{2,1,0:T(8,128)(2,1)} %get-tuple-element.10.u2_ref, bf16[192,768]{1,0:T(8,128)(2,1)} %w_out_ref.1, bf16[768,768]{1,0:T(8,128)(2,1)} %w_down_ref.1, ...), custom_call_target="tpu_custom_call" | custom-call | tf_op jit(solution)/shard_map/output/pallas_call | solution.py:542
  211.5 1.5 copy.33
  (11 shorter events, 0.1 us)
Async XLA Ops:
  3.8 2.2 %copy-start = (bf16[768,192]{0,1:T(8,128)(2,1)S(1)}, bf16[768,192]{0,1:T(8,128)(2,1)}, u32[]{:S(2)}) copy-start(bf16[768,192]{0,1:T(8,128)(2,1)} %param.16) | copy-start | bytes 884740
  4.0 2.2 %copy-start.1 = (bf16[768,192]{0,1:T(8,128)(2,1)S(1)}, bf16[768,192]{0,1:T(8,128)(2,1)}, u32[]{:S(2)}) copy-start(bf16[768,192]{0,1:T(8,128)(2,1)} %param.17) | copy-start | bytes 884740
  4.9 1.5 copy-start.2
  6.0 2.0 copy-start.5
  6.0 2.6 %copy-start.3 = (f32[768]{0:T(1024)S(1)}, f32[768]{0:T(1024)}, u32[]{:S(2)}) copy-start(f32[768]{0:T(1024)} %param.21) | copy-start | bytes 9220
  9.2 145.9 %copy-start.6 = (s32[128]{0:T(128)S(1)}, s32[128]{0:T(128)}, u32[]{:S(2)}) copy-start(s32[128]{0:T(128)} %param.29) | copy-start | bytes 1540
  155.1 13.7 %copy-start.4 = (f32[768]{0:T(1024)S(1)}, f32[768]{0:T(1024)}, u32[]{:S(2)}) copy-start(f32[768]{0:T(1024)} %param.24) | copy-start | bytes 9220

commit v2 on v1

v2 whole, which is shorter than its diff:
```python
import jax
import jax.numpy as jnp
import numpy as np
from jax import lax
from jax.experimental import pallas as pl
from jax.experimental.pallas import tpu as pltpu
from jax.sharding import PartitionSpec as P

D = 6144
HEAD_DIM = 96
ROTARY = 24
PAGE = 16
WINDOW = 128
SEQS = 8
NPAGES = 128
TOKENS = 2048
MESH = pl.DeviceIdType.MESH
F32 = jnp.float32
BF16 = jnp.bfloat16
VM = pltpu.VMEM
DMA = pltpu.SemaphoreType.DMA
FEAT = 768
HEADS2 = 192
ROT_COLS = 2 * HEADS2
QKV_PAD = 640
UNITS = 768
BLOCK = 64
OWN = 128
COLS = {"q": QKV_PAD, "u": UNITS}


class Place:
    def __init__(self):
        wide = lax.axis_index("wide")
        narrow = lax.axis_index("narrow")
        self.x, self.zl, self.c = wide // 8, (wide // 2) % 4, wide % 2
        self.y, self.zh = narrow // 2, narrow % 2
        self.wide, self.narrow = wide, narrow

    def in_wide(self, dx, dz, dc):
        return lax.rem(self.x + dx, 4) * 8 + lax.rem(self.zl + dz, 4) * 2 + lax.rem(self.c + dc, 2)

    def in_narrow(self, dy, dh):
        return lax.rem(self.y + dy, 4) * 2 + lax.rem(self.zh + dh, 2)

    def wide_peer(self, dx, dz, dc):
        return {"wide": self.in_wide(dx, dz, dc), "narrow": self.narrow}

    def narrow_peer(self, dy, dh):
        return {"wide": self.wide, "narrow": self.in_narrow(dy, dh)}


def greet(peers):
    barrier = pltpu.get_barrier_semaphore()
    for peer in peers:
        pl.semaphore_signal(barrier, inc=1, device_id=peer, device_id_type=MESH)
    pl.semaphore_wait(barrier, len(peers))


def send(src, dst, send_sem, recv_sem, peer):
    copy = pltpu.make_async_remote_copy(
        src_ref=src,
        dst_ref=dst,
        send_sem=send_sem,
        recv_sem=recv_sem,
        device_id=peer,
        device_id_type=MESH,
    )
    copy.start()
    return copy


def arrived(dst, sem, peer):
    pltpu.make_async_remote_copy(
        src_ref=dst, dst_ref=dst, send_sem=sem, recv_sem=sem, device_id=peer, device_id_type=MESH
    ).wait_recv()


WIDE_HOPS = [(0, 2, 0), (1, 0, 0), (3, 0, 0), (2, 0, 0), (0, 1, 0), (0, 3, 0), (0, 0, 1)]
NARROW_HOPS = [(dy, dh) for dy in range(4) for dh in range(2) if dy or dh]
KINDS = ("q", "u")


def slot(a, k, c):
    return (a % 4) * 8 + (k % 4) * 2 + c % 2


def project_kernel(
    lens,
    hidden_ref,
    gain_ref,
    shift_ref,
    w_query,
    w_key,
    w_value,
    w_up,
    qkv_bias_ref,
    up_bias_ref,
    qkv,
    units,
    w_qkv,
    gathered,
    stats,
    stats_part,
    tables,
    normed,
    part_q0,
    part_q1,
    part_u0,
    part_u1,
    first_q0,
    first_q1,
    first_u0,
    first_u1,
    side_q0,
    side_q1,
    side_u0,
    side_u1,
    across_q0,
    across_q1,
    across_u0,
    across_u1,
    wide_send,
    wide_recv,
    stat_send,
    stat_recv,
    sn_send,
    sn_recv,
    unit_send,
    unit_recv,
):
    parts = {"q": (part_q0, part_q1), "u": (part_u0, part_u1)}
    firsts = {"q": (first_q0, first_q1), "u": (first_u0, first_u1)}
    sides = {"q": (side_q0, side_q1), "u": (side_u0, side_u1)}
    acrosses = {"q": (across_q0, across_q1), "u": (across_u0, across_u1)}
    me = Place()
    parity = me.zl % 2
    sibling = me.wide_peer(0, 0, 1)
    greet([me.wide_peer(*hop) for hop in WIDE_HOPS] + [me.narrow_peer(*hop) for hop in NARROW_HOPS])
    open_copies = []

    counts = {"wide": 0, "stat": 0}

    def push(kind, rel, hop, own=False):
        buf, ss, rs = (
            (gathered, wide_send, wide_recv) if kind == "wide" else (stats, stat_send, stat_recv)
        )
        i = counts[kind]
        counts[kind] = i + 1
        index = me.in_wide(*rel)
        src = hidden_ref if own and kind == "wide" else buf.at[index]
        there = slot(rel[0] - hop[0], rel[1] - hop[1], rel[2] - hop[2])
        open_copies.append(send(src, buf.at[index], ss.at[i], rs.at[there], me.wide_peer(*hop)))

    def wait_block(kind, rel):
        buf, rs = (gathered, wide_recv) if kind == "wide" else (stats, stat_recv)
        arrived(buf.at[me.in_wide(*rel)], rs.at[slot(*rel)], sibling)

    def normalise(block, rel):
        index = me.in_wide(*rel)
        as_float = block.astype(F32)
        line = stats[index][0:1, :]
        lane = lax.broadcasted_iota(jnp.int32, (BLOCK, 128), 1)
        row = lax.broadcasted_iota(jnp.int32, (BLOCK, 128), 0)
        average = jnp.sum(jnp.where(lane == row, line, 0.0), axis=1, keepdims=True)
        inverse = jnp.sum(jnp.where(lane == row + BLOCK, line, 0.0), axis=1, keepdims=True)
        scaled = (as_float - average) * inverse
        owner = lax.rem(me.x + rel[0], 4) * 2 + lax.rem(me.zl + rel[1], 4) // 2
        core = lax.rem(me.c + rel[2], 2)
        for i in range(2):
            normed[i, rel[1] % 2, owner, core] = (
                scaled * gain_ref[i : i + 1, :] + shift_ref[i : i + 1, :]
            ).astype(BF16)

    own, core_hop = (0, 0, 0), (0, 0, 1)
    x_hops = [(1, 0, 0), (3, 0, 0), (2, 0, 0)]
    for hop in [(0, 2, 0)] + x_hops + [core_hop]:
        push("wide", own, hop, True)
    lanes = lax.broadcasted_iota(jnp.int32, (BLOCK, 128), 1)
    rows = lax.broadcasted_iota(jnp.int32, (BLOCK, 128), 0)
    as_float = hidden_ref[...].astype(F32)
    sums = jnp.sum(as_float, axis=1, keepdims=True)
    squares = jnp.sum(as_float * as_float, axis=1, keepdims=True)
    line = jnp.where(lanes == rows, sums, 0.0) + jnp.where(lanes == rows + BLOCK, squares, 0.0)
    stats_part[me.narrow] = jnp.broadcast_to(jnp.sum(line, axis=0, keepdims=True), (8, 128))
    for i, (dy, dh) in enumerate(NARROW_HOPS):
        mine = stats_part.at[me.narrow]
        there = ((-dy) % 4) * 2 + (-dh) % 2
        open_copies.append(send(mine, mine, sn_send.at[i], sn_recv.at[there], me.narrow_peer(dy, dh)))
    for hop in [(0, 1, 0), (0, 3, 0)]:
        push("wide", own, hop, True)
    rel = (0, 2, 0)
    wait_block("wide", rel)
    for hop in x_hops + [core_hop]:
        push("wide", rel, hop)
    for dy, dh in NARROW_HOPS:
        arrived(stats_part.at[me.in_narrow(dy, dh)], sn_recv.at[dy * 2 + dh], sibling)
    total = stats_part[0]
    for i in range(1, 8):
        total = total + stats_part[i]
    average = total[:, :BLOCK] / D
    variance = total[:, BLOCK:] / D - average * average
    stats[me.wide] = jnp.concatenate([average, lax.rsqrt(variance + 1e-05)], axis=1)
    for hop in WIDE_HOPS:
        push("stat", own, hop, True)
    normalise(hidden_ref[...], own)
    wait_block("stat", rel)
    for hop in x_hops + [core_hop]:
        push("stat", rel, hop)
    normalise(gathered[me.in_wide(*rel)], rel)

    pad = QKV_PAD - 3 * HEADS2
    qkv_bias = jnp.concatenate(
        [qkv_bias_ref[i : i + 1, :] for i in range(3)] + [jnp.zeros((1, pad), F32)], axis=1
    )
    up_bias = up_bias_ref[...].reshape(1, UNITS)
    w_qkv[...] = jnp.concatenate(
        [w_query[...], w_key[...], w_value[...], jnp.zeros((pad, FEAT), BF16)], axis=0
    ).T

    def sequence_start(token):
        end = 0
        start = token * 0
        for s in range(SEQS):
            end = end + lens[s]
            start = jnp.where(token >= end, end, start)
        return start

    def side_of(t):
        return parity if t == 0 else 1 - parity

    def first_token(t, owner):
        return owner * (2 * OWN) + side_of(t) * OWN

    def rotation_factors():
        lane = lax.broadcasted_iota(jnp.int32, (1, ROT_COLS), 1) % HEAD_DIM
        step = lane % (ROTARY // 2)
        inverses = np.power(np.float32(10000.0), (-2.0 * np.arange(12) / ROTARY).astype(np.float32))
        frequency = jnp.zeros((1, ROT_COLS), F32)
        for i in range(ROTARY // 2):
            frequency = jnp.where(step == i, F32(inverses[i]), frequency)
        for t in range(2):
            token = first_token(t, me.narrow) + lax.broadcasted_iota(jnp.int32, (OWN, 1), 0)
            position = (token - sequence_start(token)).astype(F32)
            angle = jnp.where(lane < ROTARY, position * frequency, 0.0)
            sine = jnp.sin(angle)
            tables[t, 0] = jnp.cos(angle)
            tables[t, 1] = jnp.where(lane < ROTARY // 2, -sine, 0.0)
            tables[t, 2] = jnp.where(lane < ROTARY // 2, 0.0, sine)

    def from_x(k, a):
        rel = (a, k, 0)
        for kind in ("wide", "stat"):
            wait_block(kind, rel)
            push(kind, rel, core_hop)
        normalise(gathered[me.in_wide(*rel)], rel)

    def from_sibling(ks):
        for k in ks:
            for a in (0, 1, 3, 2):
                rel = (a, k, 1)
                for kind in ("wide", "stat"):
                    wait_block(kind, rel)
                normalise(gathered[me.in_wide(*rel)], rel)

    def gather_first():
        for a in (1, 3, 2):
            from_x(0, a)
        for k in (1, 3):
            rel = (0, k, 0)
            wait_block("stat", rel)
            for hop in x_hops + [core_hop]:
                push("stat", rel, hop)
            wait_block("wide", rel)
            push("wide", rel, core_hop)
        for a in (1, 3):
            from_x(2, a)
        for k in (1, 3):
            for hop in x_hops:
                push("wide", (0, k, 0), hop)
        from_x(2, 2)
        from_sibling((0, 2))

    def gather_second():
        for k in (1, 3):
            normalise(gathered[me.in_wide(0, k, 0)], (0, k, 0))
        for k in (1, 3):
            for a in (1, 3, 2):
                from_x(k, a)
        from_sibling((1, 3))

    def multiply(kind, t):
        which, weight = (0, w_qkv) if kind == "q" else (1, w_up)
        part = parts[kind][t]

        @pl.loop(0, 4)
        def _(pair):
            rows = normed[which, t, pl.ds(pair * 2, 2)].reshape(2 * OWN, FEAT)
            product = jnp.dot(rows, weight[...], preferred_element_type=F32).astype(BF16)
            part[pl.ds(pair * 2, 2)] = product.reshape(2, OWN, COLS[kind])

    sent = {}
    up, down, across = me.narrow_peer(1, 0), me.narrow_peer(3, 0), me.narrow_peer(0, 1)
    whole, ra, rb = (0, OWN), (0, OWN // 2), (OWN // 2, OWN // 2)

    def number(u):
        return KINDS.index(u[0]) * 2 + u[1]

    def put(u, src, dst, sem, peer):
        i = sent.get(u, 0)
        sent[u] = i + 1
        n = number(u)
        open_copies.append(send(src, dst, unit_send.at[n, i], unit_recv.at[n, sem], peer))

    def got(u, dst, sem):
        arrived(dst, unit_recv.at[number(u), sem], up)

    def bufs(u):
        kind, t = u
        return parts[kind][t], firsts[kind][t], sides[kind][t], acrosses[kind][t]

    def result(u, owner, rows):
        kind, t = u
        if kind == "q":
            return qkv.at[owner * 2 + side_of(t), pl.ds(*rows)]
        return units.at[owner * 2 + side_of(t), pl.ds(*rows)]

    def scatter_first(u):
        part, first, side, _ = bufs(u)
        for h in (1, 0):
            far, nxt, prv = me.in_narrow(2, h), me.in_narrow(1, h), me.in_narrow(3, h)
            a, b = pl.ds(*ra), pl.ds(*rb)
            put(u, part.at[far, a], first.at[h, 0], 6 * h + 0, up)
            put(u, part.at[far, b], first.at[h, 1], 6 * h + 1, down)
            put(u, part.at[nxt, b], side.at[h, 0, b], 6 * h + 2, up)
            put(u, part.at[prv, a], side.at[h, 1, a], 6 * h + 3, down)

    def scatter_second(u):
        part, first, side, _ = bufs(u)
        a, b = pl.ds(*ra), pl.ds(*rb)
        for h in (1, 0):
            nxt, prv = me.in_narrow(1, h), me.in_narrow(3, h)
            got(u, first.at[h, 0], 6 * h + 0)
            part[nxt, a] = (part[nxt, a].astype(F32) + first[h, 0].astype(F32)).astype(BF16)
            put(u, part.at[nxt, a], side.at[h, 0, a], 6 * h + 4, up)
            got(u, first.at[h, 1], 6 * h + 1)
            part[prv, b] = (part[prv, b].astype(F32) + first[h, 1].astype(F32)).astype(BF16)
            put(u, part.at[prv, b], side.at[h, 1, b], 6 * h + 5, down)

    def sum_of(u, h):
        part, _, side, _ = bufs(u)
        a, b = pl.ds(*ra), pl.ds(*rb)
        got(u, side.at[h, 0, b], 6 * h + 2)
        got(u, side.at[h, 1, a], 6 * h + 3)
        got(u, side.at[h, 0, a], 6 * h + 4)
        got(u, side.at[h, 1, b], 6 * h + 5)
        own = me.in_narrow(0, h)
        return part[own].astype(F32) + side[h, 0].astype(F32) + side[h, 1].astype(F32)

    def scatter_across(u):
        zbuf = bufs(u)[3]
        zbuf[0] = sum_of(u, 1).astype(BF16)
        put(u, zbuf.at[0], zbuf.at[1], 12, across)

    def finish(u):
        kind, t = u
        zbuf = bufs(u)[3]
        summed = sum_of(u, 0)
        got(u, zbuf.at[1], 12)
        summed = summed + zbuf[1].astype(F32)
        mine = result(u, me.narrow, whole)
        if kind == "q":
            v = summed + qkv_bias
            turned = v[:, :ROT_COLS]
            turned = (
                turned * tables[t, 0]
                + pltpu.roll(turned, ROT_COLS - ROTARY // 2, 1) * tables[t, 1]
                + pltpu.roll(turned, ROTARY // 2, 1) * tables[t, 2]
            )
            qkv[me.narrow * 2 + side_of(t)] = jnp.concatenate([turned, v[:, ROT_COLS:]], axis=1).astype(BF16)
        else:
            v = summed + up_bias
            units[me.narrow * 2 + side_of(t)] = (0.5 * v * (1.0 + lax.erf(v * (0.5**0.5)))).astype(BF16)
        put(u, mine, mine, 13, across)
        put(u, mine, mine, 14, up)
        put(u, mine, mine, 15, down)

    def relay_half(u, h):
        below, above = me.in_narrow(3, h), me.in_narrow(1, h)
        got(u, result(u, below, whole), 14 + 4 * h)
        put(u, result(u, below, ra), result(u, below, ra), 16 + 4 * h, up)
        got(u, result(u, above, whole), 15 + 4 * h)
        put(u, result(u, above, rb), result(u, above, rb), 17 + 4 * h, down)

    def relay_across(u):
        block = result(u, me.in_narrow(0, 1), whole)
        got(u, block, 13)
        put(u, block, block, 18, up)
        put(u, block, block, 19, down)

    def gather_last(u):
        for h in range(2):
            far = me.in_narrow(2, h)
            got(u, result(u, far, ra), 16 + 4 * h)
            got(u, result(u, far, rb), 17 + 4 * h)

    q0, q1, u0, u1 = ("q", 0), ("q", 1), ("u", 0), ("u", 1)
    gather_first()
    multiply(*q0)
    scatter_first(q0)
    multiply(*u0)
    scatter_second(q0)
    scatter_first(u0)
    gather_second()
    rotation_factors()
    multiply(*q1)
    scatter_second(u0)
    scatter_first(q1)
    multiply(*u1)
    scatter_across(q0)
    scatter_second(q1)
    scatter_first(u1)
    finish(q0)
    scatter_across(u0)
    scatter_second(u1)
    scatter_across(q1)
    finish(u0)
    relay_half(q0, 0)
    relay_across(q0)
    finish(q1)
    scatter_across(u1)
    relay_half(u0, 0)
    relay_across(u0)
    relay_half(q0, 1)
    relay_half(q1, 0)
    finish(u1)
    relay_across(q1)
    relay_half(u0, 1)
    relay_half(q1, 1)
    relay_half(u1, 0)
    relay_across(u1)
    relay_half(u1, 1)
    for u in (q0, q1, u0, u1):
        gather_last(u)
    for copy in open_copies:
        copy.wait_send()


def attend_kernel(lens, sinks, pages, qkv_ref, out_ref, cache_ref):
    block = pl.program_id(0)
    queries, span, tail = 256, 384, 128
    total = qkv_ref.shape[0]
    first = block * queries
    width = out_ref.shape[1]

    def of_sequence(token):
        end = 0
        start = jnp.zeros_like(token)
        sink = jnp.zeros_like(token) + sinks[0]
        for s in range(8):
            end = end + lens[s]
            after = token >= end
            start = jnp.where(after, end, start)
            if s < 7:
                sink = jnp.where(after, sinks[s + 1], sink)
        return start, start + sink

    query = first + lax.broadcasted_iota(jnp.int32, (queries, 1), 0)
    start, sink_end = of_sequence(query)
    near = pl.multiple_of(jnp.maximum(first - WINDOW, 0), WINDOW)
    head_start, _ = of_sequence(first)
    far = pl.multiple_of(jnp.minimum(head_start // 16 * 16, total - tail), 16)
    near_key = near + lax.broadcasted_iota(jnp.int32, (1, span), 1)
    far_key = far + lax.broadcasted_iota(jnp.int32, (1, tail), 1)

    def allowed(key):
        return (key >= start) & (key <= query) & ((query - key < WINDOW) | (key < sink_end))

    near_ok = allowed(near_key)
    far_ok = allowed(far_key) & (far_key < near)
    mask = jnp.concatenate([near_ok, far_ok], axis=1)
    q = qkv_ref[pl.ds(first, queries), :][:, :width]
    near_rows = qkv_ref[pl.ds(near, span), :]
    far_rows = qkv_ref[pl.ds(far, tail), :]
    keys = jnp.concatenate([near_rows[:, width : 2 * width], far_rows[:, width : 2 * width]], axis=0)
    values = jnp.concatenate(
        [near_rows[:, 2 * width : 3 * width], far_rows[:, 2 * width : 3 * width]], axis=0
    )
    lane = lax.broadcasted_iota(jnp.int32, (queries, width), 1)
    result = None
    for head in range(width // HEAD_DIM):
        in_head = (lane >= head * HEAD_DIM) & (lane < (head + 1) * HEAD_DIM)
        masked_q = jnp.where(in_head, q, jnp.zeros_like(q))
        scores = lax.dot_general(
            masked_q, keys, (((1,), (1,)), ((), ())), preferred_element_type=F32
        ) * (1.0 / HEAD_DIM**0.5)
        scores = jnp.where(mask, scores, F32(-1e30))
        weights = jnp.exp(scores - jnp.max(scores, axis=1, keepdims=True))
        probs = (weights * (1.0 / jnp.sum(weights, axis=1, keepdims=True))).astype(BF16)
        got = jnp.dot(probs, values, preferred_element_type=F32)
        result = got if result is None else jnp.where(in_head, got, result)
    out_ref[...] = result.astype(BF16)
    for j in range(2):
        row = pl.multiple_of(pages[block * 2 + j] * PAGE, PAGE)
        page = qkv_ref[pl.ds(row, PAGE), :]
        cache_ref[0, j] = page[:, width : 2 * width]
        cache_ref[1, j] = page[:, 2 * width : 3 * width]


def attend(lens, sinks, pages, qkv, width):
    return pl.pallas_call(
        attend_kernel,
        out_shape=[
            jax.ShapeDtypeStruct((qkv.shape[0], width), BF16),
            jax.ShapeDtypeStruct((2, 16, PAGE, width), BF16),
        ],
        grid_spec=pltpu.PrefetchScalarGridSpec(
            num_scalar_prefetch=3,
            grid=(8,),
            in_specs=[pl.BlockSpec(qkv.shape, lambda b, *_: (0, 0))],
            out_specs=[
                pl.BlockSpec((256, width), lambda b, *_: (b, 0)),
                pl.BlockSpec((2, 2, PAGE, width), lambda b, *_: (0, b, 0, 0)),
            ],
        ),
        name="attend",
    )(lens, sinks, pages, qkv)


def output_kernel(
    att_ref,
    units_ref,
    w_out_ref,
    w_down_ref,
    hidden_ref,
    bias_ref,
    out_ref,
    products,
    core_in,
    halves,
    x_in,
    z_out,
    z_in,
    core_send,
    core_recv,
    x_send,
    x_recv,
    z_send,
    z_recv,
):
    me = Place()
    greet([me.wide_peer(*hop) for hop in WIDE_HOPS])
    open_copies = []
    sibling = me.wide_peer(0, 0, 1)
    width = out_ref.shape[1]
    order = (2, 1, 3, 0)
    for half in range(2):
        for dx in order:
            n = lax.rem(me.x + dx, 4) * 2 + half
            o = jnp.dot(units_ref[n], w_down_ref[...], preferred_element_type=F32)
            o = o + jnp.dot(att_ref[n], w_out_ref[...], preferred_element_type=F32)
            products[n] = o.astype(BF16).reshape(2, 2, 64, width)
            for j in range(2):
                i = half * 8 + dx * 2 + j
                open_copies.append(
                    send(
                        products.at[n, j, 1 - me.c], core_in.at[n, j], core_send.at[i], core_recv.at[i], sibling
                    )
                )
    for half in range(2):
        for dx in order:
            n = lax.rem(me.x + dx, 4) * 2 + half
            for j in range(2):
                arrived(core_in.at[n, j], core_recv.at[half * 8 + dx * 2 + j], sibling)
            halves[half, dx] = (products[n, :, me.c].astype(F32) + core_in[n].astype(F32)).astype(BF16)
            if dx:
                i = half * 3 + dx - 1
                there = half * 3 + (4 - dx) - 1
                open_copies.append(
                    send(
                        halves.at[half, dx], x_in.at[half, 3 - dx],
                        x_send.at[i], x_recv.at[there], me.wide_peer(dx, 0, 0),
                    )
                )
    for half in range(2):
        total = halves[half, 0].astype(F32)
        for dx in (1, 3, 2):
            arrived(x_in.at[half, dx - 1], x_recv.at[half * 3 + dx - 1], sibling)
            total = total + x_in[half, dx - 1].astype(F32)
        z_out[half] = total.astype(BF16)
        for j in range(2):
            to = half * 2 + j
            peer = {"wide": me.x * 8 + to * 2 + me.c, "narrow": me.narrow}

            @pl.when(me.zl != to)
            def _():
                send(z_out.at[half, j], z_in.at[me.zl], z_send.at[to], z_recv.at[me.zl], peer)

    total = z_out[me.zl // 2, me.zl % 2].astype(F32) + hidden_ref[...].astype(F32) + bias_ref[...].reshape(1, FEAT)
    for k in range(1, 4):
        source = lax.rem(me.zl + k, 4)
        arrived(z_in.at[source], z_recv.at[source], sibling)
        total = total + z_in[source].astype(F32)
    out_ref[...] = total.astype(BF16)
    for copy in open_copies:
        copy.wait_send()
    for k in range(1, 4):
        to = lax.rem(me.zl + k, 4)
        pltpu.make_async_remote_copy(
            src_ref=z_out.at[to // 2, to % 2], dst_ref=z_in.at[me.zl], send_sem=z_send.at[to],
            recv_sem=z_recv.at[me.zl], device_id=me.wide_peer(0, k, 0), device_id_type=MESH,
        ).wait_send()


def output(att, units, w_out, w_down, hidden, bias):
    width = hidden.shape[1]
    return pl.pallas_call(
        output_kernel,
        out_shape=jax.ShapeDtypeStruct(hidden.shape, BF16),
        in_specs=[pl.BlockSpec(memory_space=VM)] * 6,
        out_specs=pl.BlockSpec(memory_space=VM),
        scratch_shapes=[
            VM((8, 2, 2, 64, width), BF16),
            VM((8, 2, 64, width), BF16),
            VM((2, 4, 2, 64, width), BF16),
            VM((2, 3, 2, 64, width), BF16),
            VM((2, 2, 64, width), BF16),
            VM((4, 64, width), BF16),
            DMA((16,)),
            DMA((16,)),
            DMA((6,)),
            DMA((6,)),
            DMA((4,)),
            DMA((4,)),
        ],
        compiler_params=pltpu.CompilerParams(
            collective_id=1, has_side_effects=True, vmem_limit_bytes=56 << 20
        ),
        name="output",
    )(att, units, w_out, w_down, hidden, bias)


def local(
    hidden_in,
    w_query,
    w_key,
    w_value,
    qkv_bias,
    w_up,
    up_bias,
    w_attn_out,
    w_down,
    out_bias,
    norm_gain,
    norm_bias,
    seq_lens,
    sink_count,
    page_table,
):
    vmem = pl.BlockSpec(memory_space=VM)
    smem = pl.BlockSpec(memory_space=pltpu.SMEM)
    both = (QKV_PAD, QKV_PAD, UNITS, UNITS)
    qkv, units = pl.pallas_call(
        project_kernel,
        out_shape=[jax.ShapeDtypeStruct((TOKENS // OWN, OWN, c), BF16) for c in (QKV_PAD, UNITS)],
        in_specs=[smem] + [vmem] * 9,
        out_specs=[vmem] * 2,
        scratch_shapes=[
            VM((FEAT, QKV_PAD), BF16),
            VM((32, BLOCK, FEAT), BF16),
            VM((32, 8, 128), F32),
            VM((8, 8, 128), F32),
            VM((2, 3, OWN, ROT_COLS), F32),
            VM((2, 2, 8, 2, BLOCK, FEAT), BF16),
        ]
        + [VM((8, OWN, c), BF16) for c in both]
        + [VM((2, 2, OWN // 2, c), BF16) for c in both]
        + [VM((2, 2, OWN, c), BF16) for c in both]
        + [VM((2, OWN, c), BF16) for c in both]
        + [
            DMA((31,)),
            DMA((32,)),
            DMA((31,)),
            DMA((32,)),
            DMA((7,)),
            DMA((8,)),
            DMA((4, 22)),
            DMA((4, 22)),
        ],
        compiler_params=pltpu.CompilerParams(
            collective_id=0, has_side_effects=True, vmem_limit_bytes=56 << 20
        ),
        name="project",
    )(
        seq_lens,
        hidden_in,
        norm_gain,
        norm_bias,
        w_query.T,
        w_key.T,
        w_value.T,
        w_up,
        qkv_bias,
        up_bias,
    )
    slot_ids = lax.axis_index("narrow") * 16 + jnp.arange(16, dtype=jnp.int32)
    matches = (page_table[None, :] == slot_ids[:, None]).astype(jnp.int32)
    source_page = jnp.sum(matches * jnp.arange(NPAGES, dtype=jnp.int32)[None, :], axis=1)
    attended, cache = attend(seq_lens, sink_count, source_page, qkv.reshape(TOKENS, QKV_PAD), HEADS2)
    hidden_out = output(
        attended.reshape(8, 2 * OWN, HEADS2), units.reshape(8, 2 * OWN, UNITS), w_attn_out, w_down, hidden_in, out_bias
    )
    return (hidden_out, cache)


def solution(mesh):
    in_specs = (
        P("wide", "narrow"),
        P("narrow", "wide"),
        P("narrow", "wide"),
        P("narrow", "wide"),
        P(None, "wide"),
        P("narrow", "wide"),
        P("wide"),
        P("wide", "narrow"),
        P("wide", "narrow"),
        P("narrow"),
        P(None, "narrow"),
        P(None, "narrow"),
        P(),
        P(),
        P(),
    )
    out_specs = (P("wide", "narrow"), P(None, "narrow", None, "wide"))
    return jax.shard_map(local, mesh=mesh, in_specs=in_specs, out_specs=out_specs, check_vma=False)
```

time: 216 us -> 198 us (0.917)
  Pallas kernels: 201 us -> 191 us
  local copies, waits for them, and re-layouts: 7.44 us -> 1.54 us
  other arithmetic: 3.87 us -> 1.35 us
    pallas_call x1, Pallas kernels: 146 us -> 139 us  [local(): pl.pallas_call(project_kernel, out_shape=[jax.ShapeDtypeStruct((TOKENS //...]
    pallas_call x1, Pallas kernels: 42.1 us -> 38.2 us  [output(): pl.pallas_call(output_kernel, out_shape=jax.ShapeDtypeStruct(hidden.shape...]
    concatenate x7 -> x0, local copies, waits for them, and re-layouts: 3.53 us -> none  [the longest x3 2.71 us: spread(): jnp.concatenate([jnp.tile(head, (1, 4)), jnp.full((256, QKV_PAD - 4 * HEA...]
where the time goes in v2:
time: 198 us; the launch traced here: 194 us
  Pallas kernels  191 us (96%)
    pallas_call x1, Pallas kernels, local(): pl.pallas_call(project_kernel, out_shape=[jax.ShapeDtypeStruct((TOKENS //...  139 us
    pallas_call x1, Pallas kernels, output(): pl.pallas_call(output_kernel, out_shape=jax.ShapeDtypeStruct(hidden.shape...  38.2 us
    pallas_call x1, Pallas kernels, attend(): pl.pallas_call(attend_kernel, out_shape=[jax.ShapeDtypeStruct((qkv.shape[...  13 us

profile of v2, /device:TPU:8, one launch (start us, length us, event | category | flops | bytes accessed | tf_op | source)
XLA Modules:
  0.0 194.1 jit_solution(4155101206506265782)
XLA Ops:
  0.6 1.4 select_reduce_fusion.pages
  2.0 139.3 %project.1 = (bf16[16,128,640]{2,1,0:T(8,128)(2,1)}, bf16[16,128,768]{2,1,0:T(8,128)(2,1)}) custom-call(s32[8]{0:T(128)} %lens.3, bf16[64,768]{1,0:T(8,128)(2,1)} %hidden_ref.3, f32[2,768]{1,0:T(2,128)} %gain_ref.1, f32[2,768]{1,0:T(2,128)} %shift_ref.1, bf16[192,768]{1,0:T(8,128)(2,1)} %bitcast.9, bf16[192,768]{1,0:T(8,128)(2,1)} %bitcast.10, ...), custom_call_target="tpu_custom_call" | custom-call | tf_op jit(solution)/shard_map/project/pallas_call | solution.py:663
  141.3 13.0 %attend.1 = (bf16[2048,192]{1,0:T(8,128)(2,1)}, bf16[2,16,16,192]{3,2,1,0:T(8,128)(2,1)}) custom-call(s32[8]{0:T(128)} %lens.3, s32[8]{0:T(128)} %sinks.1, s32[16]{0:T(128)} %select_reduce_fusion.pages, bf16[2048,640]{1,0:T(8,128)(2,1)} %bitcast.7), custom_call_target="tpu_custom_call" | custom-call | tf_op jit(solution)/shard_map/attend/pallas_call | solution.py:511
  154.3 38.2 %output.1 = bf16[64,768]{1,0:T(8,128)(2,1)} custom-call(bf16[8,256,192]{2,1,0:T(8,128)(2,1)} %bitcast.8, bf16[8,256,768]{2,1,0:T(8,128)(2,1)} %bitcast.6, bf16[192,768]{1,0:T(8,128)(2,1)} %w_out_ref.1, bf16[768,768]{1,0:T(8,128)(2,1)} %w_down_ref.1, bf16[64,768]{1,0:T(8,128)(2,1)} %hidden_ref.3, f32[768]{0:T(1024)} %bias_ref.1), custom_call_target="tpu_custom_call" | custom-call | tf_op jit(solution)/shard_map/output/pallas_call | solution.py:617
  192.5 1.5 copy.18
  (1 shorter events, 0.0 us)

commit v3 on v2

--- a/solution.py
+++ b/solution.py
@@ -473,12 +473,9 @@
     near_key = near + lax.broadcasted_iota(jnp.int32, (1, span), 1)
     far_key = far + lax.broadcasted_iota(jnp.int32, (1, tail), 1)
 
-    def allowed(key):
-        return (key >= start) & (key <= query) & ((query - key < WINDOW) | (key < sink_end))
-
-    near_ok = allowed(near_key)
-    far_ok = allowed(far_key) & (far_key < near)
-    mask = jnp.concatenate([near_ok, far_ok], axis=1)
+    far_key = jnp.where(far_key < near, far_key, 2 * total)
+    key = jnp.concatenate([near_key, far_key], axis=1)
+    mask = (key <= query) & (key >= start) & ((key > query - WINDOW) | (key < sink_end))
     q = qkv_ref[pl.ds(first, queries), :][:, :width]
     near_rows = qkv_ref[pl.ds(near, span), :]
     far_rows = qkv_ref[pl.ds(far, tail), :]
@@ -554,34 +551,44 @@
     sibling = me.wide_peer(0, 0, 1)
     width = out_ref.shape[1]
     order = (2, 1, 3, 0)
-    for half in range(2):
-        for dx in order:
-            n = lax.rem(me.x + dx, 4) * 2 + half
-            o = jnp.dot(units_ref[n], w_down_ref[...], preferred_element_type=F32)
-            o = o + jnp.dot(att_ref[n], w_out_ref[...], preferred_element_type=F32)
-            products[n] = o.astype(BF16).reshape(2, 2, 64, width)
-            for j in range(2):
-                i = half * 8 + dx * 2 + j
-                open_copies.append(
-                    send(
-                        products.at[n, j, 1 - me.c], core_in.at[n, j], core_send.at[i], core_recv.at[i], sibling
-                    )
+
+    def multiply(half, dx):
+        n = lax.rem(me.x + dx, 4) * 2 + half
+        o = jnp.dot(units_ref[n], w_down_ref[...], preferred_element_type=F32)
+        o = o + jnp.dot(att_ref[n], w_out_ref[...], preferred_element_type=F32)
+        products[n] = o.astype(BF16).reshape(2, 2, 64, width)
+        for j in range(2):
+            i = half * 8 + dx * 2 + j
+            open_copies.append(
+                send(
+                    products.at[n, j, 1 - me.c], core_in.at[n, j], core_send.at[i], core_recv.at[i], sibling
                 )
-    for half in range(2):
-        for dx in order:
-            n = lax.rem(me.x + dx, 4) * 2 + half
-            for j in range(2):
-                arrived(core_in.at[n, j], core_recv.at[half * 8 + dx * 2 + j], sibling)
-            halves[half, dx] = (products[n, :, me.c].astype(F32) + core_in[n].astype(F32)).astype(BF16)
-            if dx:
-                i = half * 3 + dx - 1
-                there = half * 3 + (4 - dx) - 1
-                open_copies.append(
-                    send(
-                        halves.at[half, dx], x_in.at[half, 3 - dx],
-                        x_send.at[i], x_recv.at[there], me.wide_peer(dx, 0, 0),
-                    )
+            )
+
+    def pass_on(half, dx):
+        n = lax.rem(me.x + dx, 4) * 2 + half
+        for j in range(2):
+            arrived(core_in.at[n, j], core_recv.at[half * 8 + dx * 2 + j], sibling)
+        halves[half, dx] = (products[n, :, me.c].astype(F32) + core_in[n].astype(F32)).astype(BF16)
+        if dx:
+            i = half * 3 + dx - 1
+            there = half * 3 + (4 - dx) - 1
+            open_copies.append(
+                send(
+                    halves.at[half, dx],
+                    x_in.at[half, 3 - dx],
+                    x_send.at[i],
+                    x_recv.at[there],
+                    me.wide_peer(dx, 0, 0),
                 )
+            )
+
+    steps = [(half, dx) for half in range(2) for dx in order]
+    for i, step in enumerate(steps):
+        multiply(*step)
+        if i:
+            pass_on(*steps[i - 1])
+    pass_on(*steps[-1])
     for half in range(2):
         total = halves[half, 0].astype(F32)
         for dx in (1, 3, 2):

time: 198 us -> 195 us (0.985)
  Pallas kernels: 191 us -> 188 us
    pallas_call x1, Pallas kernels: 38.2 us -> 35.9 us  [output(): pl.pallas_call(output_kernel, out_shape=jax.ShapeDtypeStruct(hidden.shape...]
where the time goes in v3:
time: 195 us; the launch traced here: 192 us
  Pallas kernels  188 us (96%)
    pallas_call x1, Pallas kernels, local(): pl.pallas_call(project_kernel, out_shape=[jax.ShapeDtypeStruct((TOKENS //...  139 us
    pallas_call x1, Pallas kernels, output(): pl.pallas_call(output_kernel, out_shape=jax.ShapeDtypeStruct(hidden.shape...  35.9 us
    pallas_call x1, Pallas kernels, attend(): pl.pallas_call(attend_kernel, out_shape=[jax.ShapeDtypeStruct((qkv.shape[...  13 us

profile of v3, /device:TPU:8, one launch (start us, length us, event | category | flops | bytes accessed | tf_op | source)
XLA Modules:
  0.0 191.8 jit_solution(16315025859081695035)
XLA Ops:
  0.6 1.4 select_reduce_fusion.pages
  2.0 139.3 %project.1 = (bf16[16,128,640]{2,1,0:T(8,128)(2,1)}, bf16[16,128,768]{2,1,0:T(8,128)(2,1)}) custom-call(s32[8]{0:T(128)} %lens.3, bf16[64,768]{1,0:T(8,128)(2,1)} %hidden_ref.3, f32[2,768]{1,0:T(2,128)} %gain_ref.1, f32[2,768]{1,0:T(2,128)} %shift_ref.1, bf16[192,768]{1,0:T(8,128)(2,1)} %bitcast.9, bf16[192,768]{1,0:T(8,128)(2,1)} %bitcast.10, ...), custom_call_target="tpu_custom_call" | custom-call | tf_op jit(solution)/shard_map/project/pallas_call | solution.py:670
  141.3 13.0 %attend.1 = (bf16[2048,192]{1,0:T(8,128)(2,1)}, bf16[2,16,16,192]{3,2,1,0:T(8,128)(2,1)}) custom-call(s32[8]{0:T(128)} %lens.3, s32[8]{0:T(128)} %sinks.1, s32[16]{0:T(128)} %select_reduce_fusion.pages, bf16[2048,640]{1,0:T(8,128)(2,1)} %bitcast.7), custom_call_target="tpu_custom_call" | custom-call | tf_op jit(solution)/shard_map/attend/pallas_call | solution.py:508
  154.3 35.9 %output.1 = bf16[64,768]{1,0:T(8,128)(2,1)} custom-call(bf16[8,256,192]{2,1,0:T(8,128)(2,1)} %bitcast.8, bf16[8,256,768]{2,1,0:T(8,128)(2,1)} %bitcast.6, bf16[192,768]{1,0:T(8,128)(2,1)} %w_out_ref.1, bf16[768,768]{1,0:T(8,128)(2,1)} %w_down_ref.1, bf16[64,768]{1,0:T(8,128)(2,1)} %hidden_ref.3, f32[768]{0:T(1024)} %bias_ref.1), custom_call_target="tpu_custom_call" | custom-call | tf_op jit(solution)/shard_map/output/pallas_call | solution.py:624
  190.2 1.5 copy.18
  (1 shorter events, 0.0 us)
